TPU v7x, 512 devices: a whole 4x4x16 slice. The times are simulated.
512 devices in a mesh: req: 8 (over z_lo), section: 2 (over core), seq: 8 (over z_hi, y), tp: 4 (over x).
Axes of the slice: x: 4, y: 4, z: 16 (z_hi: 2, z_lo: 8; z = z_hi * 8 + z_lo), core: 2. Of those that a mesh axis runs over, the one named last changes fastest.
Arguments:
- hidden: bfloat16 [8192, 1536], P(('req', 'seq'), 'tp'), parts along dimension 0, may hold values from -2.5 to 2.5
- latent: float32 [8192, 64], P(('req', 'seq'), ('section', 'tp')), parts along dimension 0, may hold values from -6 to 6
- w_qkv: bfloat16 [2, 1536, 3, 1536], P('section', 'seq', None, 'tp'), may hold values from -0.15625 to 0.15625
- w_out: bfloat16 [2, 1536, 1536], P('section', 'tp'), may hold values from -0.625 to 0.625
- modulation: float32 [2, 3, 1536], P('section'), may hold values from -3 to 3
- final_mod: float32 [2, 1536], replicated, may hold values from -3 to 3
- w_final: bfloat16 [1536, 64], P(None, ('section', 'tp')), may hold values from -0.15625 to 0.15625
- stale_kv: bfloat16 [2, 2, 8192, 1536], P('section', None, ('req', 'seq'), 'tp'), parts along dimension 2, may hold values from -6 to 6
- text_kv: bfloat16 [2, 2, 1232, 1536], P('section', None, 'req', 'tp'), parts along dimension 2, as said below
- text_len: int32 [8], P('req'), parts along dimension 0, may hold values from 77 to 154
- patch_order: int32 [64, 4], P('req'), parts along dimension 0, may hold values from 0 to 3, each once within a row
- step_size: float32 [1], replicated, may hold values from -0.6 to -0.1
Outputs:
- latent_next: float32 [8192, 64], P(('req', 'seq'), ('section', 'tp')), parts along dimension 0
- new_kv: bfloat16 [2, 2, 8192, 1536], P('section', None, ('req', 'seq'), 'tp'), parts along dimension 2
There are 8 independent parts, one for each index of `req`. A program takes and returns all parts, laid end to end along the dimension named above; an argument that names none is the same for every part. Nothing has to cross between parts.
Inputs may be any that keep to these rules, and one draw needn't show every extreme that they name: Text tokens 0 to text_len - 1 are live, the rest of the 154 slots are padding. `patch_order`: each row is an ordering of the 4 patches of one index of seq. `text_kv`: keys and values of the text tokens.
All inputs are finite; a program needn't handle non-finite values.
Results may differ from a plain program's by a relative error of at most 0.015.
The roundings to bfloat16 on the way count: a program that leaves them out, or rounds other values in their place, can miss the bound.
Values may be sent and summed in bfloat16 or wider, within the bound.
A program may use at most 64 MiB of HBM per device.

v0:
```python
import jax
import jax.numpy as jnp
from jax import lax
from jax.sharding import PartitionSpec as P

HEAD = 64
MICRO = 4


def from_behind(value, axis, steps):
    count = lax.axis_size(axis)
    leading, last = (max(0, -steps), min(count, count - steps))
    return lax.ppermute(value, axis, [(source, source + steps) for source in range(leading, last)])


def layer_norm(row_block):
    row_block = row_block.astype(jnp.float32)
    center = row_block - jnp.mean(row_block, axis=-1, keepdims=True)
    spread = jnp.mean(center * center, axis=-1, keepdims=True)
    return center * lax.rsqrt(spread + 1e-06)


def modulate(row_block, shift_vec, scale_vec):
    return (layer_norm(row_block) * (1.0 + scale_vec) + shift_vec).astype(jnp.bfloat16)


def attend(queries, all_keys, all_values, text_keys, text_values, live_mask):
    factor = HEAD ** (-0.5)
    scores = (
        jnp.einsum("rhe,khe->hrk", queries, all_keys, preferred_element_type=jnp.float32) * factor
    )
    text_scores = (
        jnp.einsum("rhe,khe->hrk", queries, text_keys, preferred_element_type=jnp.float32) * factor
    )
    text_scores = jnp.where(live_mask[None, None, :], text_scores, -jnp.inf)
    peak_score = jnp.maximum(
        jnp.max(scores, axis=-1, keepdims=True), jnp.max(text_scores, axis=-1, keepdims=True)
    )
    weights = jnp.exp(scores - peak_score)
    text_weights = jnp.exp(text_scores - peak_score)
    total_mass = jnp.sum(weights, axis=-1, keepdims=True) + jnp.sum(
        text_weights, axis=-1, keepdims=True
    )
    prob_img = (weights / total_mass).astype(jnp.bfloat16)
    text_probs = (text_weights / total_mass).astype(jnp.bfloat16)
    attended = jnp.einsum("hrk,khe->rhe", prob_img, all_values, preferred_element_type=jnp.float32)
    attended = attended + jnp.einsum(
        "hrk,khe->rhe", text_probs, text_values, preferred_element_type=jnp.float32
    )
    return attended.astype(jnp.bfloat16).reshape(queries.shape[0], -1)


def take_fresh(new_kv_rows, column, is_valid, buffer, micro_ids):
    arrived = lax.all_gather(new_kv_rows[None], "seq", axis=0, tiled=True)
    hit_mask = (column[:, None] == micro_ids[None, :]) & is_valid
    return jnp.where(hit_mask[:, None, :, None, None], arrived[:, :, None], buffer)


def body(
    hidden,
    latent,
    w_qkv,
    w_out,
    modulation,
    final_mod,
    w_final,
    stale_kv,
    text_kv,
    text_len,
    patch_order,
    step_size,
):
    section_id = lax.axis_index("section")
    seq_id = lax.axis_index("seq")
    tp_id = lax.axis_index("tp")
    row_count, local_width = hidden.shape
    full_width = modulation.shape[2]
    patch_rows = row_count // MICRO
    seq_count = patch_order.shape[0]
    heads_here = local_width // HEAD
    shift_vec = modulation[0, 0]
    scale_vec = modulation[0, 1]
    gate_vec = modulation[0, 2]
    gate_here = lax.dynamic_slice_in_dim(gate_vec, tp_id * local_width, local_width)
    projection = lax.all_gather(w_qkv[0], "seq", axis=0, tiled=True).reshape(
        full_width, 3 * local_width
    )
    out_proj = w_out[0]
    text_keys = text_kv[0, 0].reshape(-1, heads_here, HEAD)
    text_values = text_kv[0, 1].reshape(-1, heads_here, HEAD)
    live_mask = jnp.arange(text_kv.shape[2], dtype=jnp.int32) < text_len[0]
    micro_ids = jnp.arange(MICRO, dtype=jnp.int32)
    seq_ids = jnp.arange(seq_count, dtype=jnp.int32)
    buffer = lax.all_gather(stale_kv, "seq", axis=0, tiled=True).reshape(
        seq_count, 2, MICRO, patch_rows, local_width
    )
    entry_blocks = hidden.reshape(MICRO, patch_rows, local_width)
    carried = jnp.zeros((patch_rows, local_width), jnp.bfloat16)
    finished = jnp.zeros((MICRO, patch_rows, local_width), jnp.bfloat16)
    for tick_index in range(MICRO + 1):
        micro_step = tick_index - section_id
        is_valid = (micro_step >= 0) & (micro_step < MICRO)
        clamped = jnp.clip(micro_step, 0, MICRO - 1)
        column = jnp.sum(jnp.where(micro_ids[None, :] == clamped, patch_order, 0), axis=1)
        my_patch = jnp.sum(jnp.where(seq_ids == seq_id, column, 0))
        picked = micro_ids == my_patch
        own_rows = lax.dynamic_index_in_dim(entry_blocks, my_patch, 0, keepdims=False)
        current = jnp.where(section_id == 0, own_rows, carried)
        full_rows = lax.all_gather(current, "tp", axis=1, tiled=True)
        normed = modulate(full_rows, shift_vec, scale_vec)
        joined = jnp.dot(normed, projection, preferred_element_type=jnp.float32).astype(
            jnp.bfloat16
        )
        queries = joined[:, :local_width].reshape(patch_rows, heads_here, HEAD)
        new_kv_rows = jnp.stack(
            [joined[:, local_width : 2 * local_width], joined[:, 2 * local_width :]]
        )
        buffer = take_fresh(new_kv_rows, column, is_valid, buffer, micro_ids)
        all_keys = buffer[:, 0].reshape(-1, heads_here, HEAD)
        all_values = buffer[:, 1].reshape(-1, heads_here, HEAD)
        attended = attend(queries, all_keys, all_values, text_keys, text_values, live_mask)
        partial_value = jnp.dot(attended, out_proj, preferred_element_type=jnp.float32)
        branch = lax.psum_scatter(partial_value, "tp", scatter_dimension=1, tiled=True)
        updated = (current.astype(jnp.float32) + gate_here * branch).astype(jnp.bfloat16)
        carried = from_behind(updated, "section", 1)
        finished = jnp.where((picked & is_valid)[:, None, None], updated[None], finished)
    returned = from_behind(finished, "section", -1)
    last_rows = jnp.where(section_id == 1, finished, returned).reshape(row_count, local_width)
    last_rows = lax.all_gather(last_rows, "tp", axis=1, tiled=True)
    final = modulate(last_rows, final_mod[0], final_mod[1])
    velocity = jnp.dot(final, w_final, preferred_element_type=jnp.float32)
    latent_next = latent + step_size[0] * velocity
    kv_next = lax.dynamic_index_in_dim(buffer, seq_id, 0, keepdims=False).reshape(
        1, 2, row_count, local_width
    )
    return (latent_next, kv_next)


def solution(mesh):
    return jax.shard_map(
        body,
        mesh=mesh,
        in_specs=(
            P(("req", "seq"), "tp"),
            P(("req", "seq"), ("section", "tp")),
            P("section", "seq", None, "tp"),
            P("section", "tp", None),
            P("section", None, None),
            P(),
            P(None, ("section", "tp")),
            P("section", None, ("req", "seq"), "tp"),
            P("section", None, "req", "tp"),
            P("req"),
            P("req", None),
            P(),
        ),
        out_specs=(P(("req", "seq"), ("section", "tp")), P("section", None, ("req", "seq"), "tp")),
        check_vma=False,
    )
```

profile of v0, /device:TPU:8, one launch (start us, length us, event | category | flops | bytes accessed | tf_op | source)
XLA Modules:
  0.0 890.9 jit_solution(9722535990750475162)
XLA Ops:
  16.4 12.3 %all-gather = bf16[1,32,1536]{2,1,0:T(8,128)(2,1)S(1)} all-gather(bf16[1,32,384]{2,1,0:T(8,128)(2,1)S(1)} %dynamic-slice_select_fusion), channel_id=2, replica_groups=mesh['req'=8,'section'=2,'seq'=8,'tp'=4] {'tp'}, dimensions={2}, use_global_device_ids=true | all-gather | bytes 122880 | tf_op jit(solution)/shard_map/all_gather | solution.py:109
  30.3 143.6 %all-gather.12.cloned.1.call-done = bf16[1,1536,3,384]{3,1,2,0:T(8,128)(2,1)} async-done(((bf16[1,192,3,384]{3,1,2,0:T(8,128)(2,1)}), bf16[1,1536,3,384]{3,1,2,0:T(8,128)(2,1)}) %all-gather.12.cloned.1.call-update) | async-done | bytes 3538960 | tf_op jit(solution)/shard_map/all_gather | solution.py:85
  173.9 6.1 copy.101
  183.2 54.6 %all-gather.2 = bf16[16,32,384]{2,1,0:T(8,128)(2,1)S(1)} all-gather(bf16[2,32,384]{2,1,0:T(8,128)(2,1)S(1)} %pad_maximum_fusion), channel_id=4, replica_groups=mesh['req'=8,'section'=2,'seq'=8,'tp'=4] {'seq'}, dimensions={0}, use_global_device_ids=true | all-gather | bytes 442368 | tf_op jit(solution)/shard_map/all_gather | solution.py:54
  237.8 38.7 %all-gather.10.cloned.1.call-done = bf16[8,2,128,384]{3,2,1,0:T(8,128)(2,1)} async-done(((bf16[1,2,128,384]{3,2,1,0:T(8,128)(2,1)}), bf16[8,2,128,384]{3,2,1,0:T(8,128)(2,1)}) %all-gather.10.cloned.1.call-update) | async-done | bytes 1572880 | tf_op jit(solution)/shard_map/all_gather | solution.py:94
  294.6 21.9 %reduce-scatter.6.cloned.1.call-done = f32[32,384]{1,0:T(8,128)} async-done(((f32[32,1536]{1,0:T(8,128)}), f32[32,384]{1,0:T(8,128)}) %reduce-scatter.6.cloned.1.call-update) | async-done | bytes 49168 | tf_op jit(solution)/shard_map/reduce_scatter | solution.py:123
  321.2 12.0 %all_gather.43 = bf16[32,1536]{1,0:T(8,128)(2,1)S(1)} all-gather(bf16[32,384]{1,0:T(8,128)(2,1)S(1)} %bitcast_select_fusion), channel_id=1, replica_groups=mesh['req'=8,'section'=2,'seq'=8,'tp'=4] {'tp'}, dimensions={1}, use_global_device_ids=true | all-gather | bytes 122880 | tf_op jit(solution)/shard_map/all_gather | solution.py:109
  337.5 65.7 %all-gather.3 = bf16[16,32,384]{2,1,0:T(8,128)(2,1)S(1)} all-gather(bf16[2,32,384]{2,1,0:T(8,128)(2,1)S(1)} %pad_maximum_fusion.1), channel_id=5, replica_groups=mesh['req'=8,'section'=2,'seq'=8,'tp'=4] {'seq'}, dimensions={0}, use_global_device_ids=true | all-gather | bytes 442368 | tf_op jit(solution)/shard_map/all_gather | solution.py:54
  405.3 3.7 reshape_squeeze.41
  416.1 3.7 reshape_squeeze.40
  427.5 25.8 %reduce-scatter.8.cloned.1.call-done = f32[32,384]{1,0:T(8,128)} async-done(((f32[32,1536]{1,0:T(8,128)}), f32[32,384]{1,0:T(8,128)}) %reduce-scatter.8.cloned.1.call-update) | async-done | bytes 49168 | tf_op jit(solution)/shard_map/reduce_scatter | solution.py:123
  460.7 12.0 %all_gather.45 = bf16[32,1536]{1,0:T(8,128)(2,1)S(1)} all-gather(bf16[32,384]{1,0:T(8,128)(2,1)S(1)} %bitcast_select_fusion.1), channel_id=1, replica_groups=mesh['req'=8,'section'=2,'seq'=8,'tp'=4] {'tp'}, dimensions={1}, use_global_device_ids=true | all-gather | bytes 122880 | tf_op jit(solution)/shard_map/all_gather | solution.py:109
  476.9 65.4 %all-gather.4 = bf16[16,32,384]{2,1,0:T(8,128)(2,1)S(1)} all-gather(bf16[2,32,384]{2,1,0:T(8,128)(2,1)S(1)} %pad_maximum_fusion.2), channel_id=6, replica_groups=mesh['req'=8,'section'=2,'seq'=8,'tp'=4] {'seq'}, dimensions={0}, use_global_device_ids=true | all-gather | bytes 442368 | tf_op jit(solution)/shard_map/all_gather | solution.py:54
  545.0 3.7 reshape_squeeze.43
  555.8 3.7 reshape_squeeze.42
  567.2 25.8 %reduce-scatter.10.cloned.1.call-done = f32[32,384]{1,0:T(8,128)} async-done(((f32[32,1536]{1,0:T(8,128)}), f32[32,384]{1,0:T(8,128)}) %reduce-scatter.10.cloned.1.call-update) | async-done | bytes 49168 | tf_op jit(solution)/shard_map/reduce_scatter | solution.py:123
  600.2 12.2 %all_gather.47 = bf16[32,1536]{1,0:T(8,128)(2,1)S(1)} all-gather(bf16[32,384]{1,0:T(8,128)(2,1)S(1)} %bitcast_select_fusion.2), channel_id=1, replica_groups=mesh['req'=8,'section'=2,'seq'=8,'tp'=4] {'tp'}, dimensions={1}, use_global_device_ids=true | all-gather | bytes 122880 | tf_op jit(solution)/shard_map/all_gather | solution.py:109
  616.6 65.3 %all-gather.5 = bf16[16,32,384]{2,1,0:T(8,128)(2,1)S(1)} all-gather(bf16[2,32,384]{2,1,0:T(8,128)(2,1)S(1)} %pad_maximum_fusion.3), channel_id=7, replica_groups=mesh['req'=8,'section'=2,'seq'=8,'tp'=4] {'seq'}, dimensions={0}, use_global_device_ids=true | all-gather | bytes 442368 | tf_op jit(solution)/shard_map/all_gather | solution.py:54
  696.0 3.7 reshape_squeeze.44
  709.9 23.3 %reduce-scatter.12.cloned.1.call-done = f32[32,384]{1,0:T(8,128)} async-done(((f32[32,1536]{1,0:T(8,128)}), f32[32,384]{1,0:T(8,128)}) %reduce-scatter.12.cloned.1.call-update) | async-done | bytes 49168 | tf_op jit(solution)/shard_map/reduce_scatter | solution.py:123
  740.3 12.0 %all_gather.49 = bf16[32,1536]{1,0:T(8,128)(2,1)S(1)} all-gather(bf16[32,384]{1,0:T(8,128)(2,1)S(1)} %bitcast_select_fusion.3), channel_id=1, replica_groups=mesh['req'=8,'section'=2,'seq'=8,'tp'=4] {'tp'}, dimensions={1}, use_global_device_ids=true | all-gather | bytes 122880 | tf_op jit(solution)/shard_map/all_gather | solution.py:109
  756.6 65.5 %all-gather.6 = bf16[16,32,384]{2,1,0:T(8,128)(2,1)S(1)} all-gather(bf16[2,32,384]{2,1,0:T(8,128)(2,1)S(1)} %pad_maximum_fusion.4), channel_id=8, replica_groups=mesh['req'=8,'section'=2,'seq'=8,'tp'=4] {'seq'}, dimensions={0}, use_global_device_ids=true | all-gather | bytes 442368 | tf_op jit(solution)/shard_map/all_gather | solution.py:54
  839.1 24.4 %reduce-scatter.14.cloned.1.call-done = f32[32,384]{1,0:T(8,128)} async-done(((f32[32,1536]{1,0:T(8,128)}), f32[32,384]{1,0:T(8,128)}) %reduce-scatter.14.cloned.1.call-update) | async-done | bytes 49168 | tf_op jit(solution)/shard_map/reduce_scatter | solution.py:123
  869.3 13.4 %all_gather.51 = bf16[128,1536]{1,0:T(8,128)(2,1)S(1)} all-gather(bf16[128,384]{1,0:T(8,128)(2,1)S(1)} %bitcast.206), channel_id=1, replica_groups=mesh['req'=8,'section'=2,'seq'=8,'tp'=4] {'tp'}, dimensions={1}, use_global_device_ids=true | all-gather | bytes 491520 | tf_op jit(solution)/shard_map/all_gather | solution.py:129
  (298 shorter events, 146.5 us)
Async XLA Ops:
  7.2 285.0 %copy-start = (bf16[1,384,1536]{2,1,0:T(8,128)(2,1)S(1)}, bf16[1,384,1536]{2,1,0:T(8,128)(2,1)}, u32[]{:S(2)}) copy-start(bf16[1,384,1536]{2,1,0:T(8,128)(2,1)} %param.15) | copy-start | bytes 3538948
  7.2 166.7 %all-gather.12.cloned.1.call-start = ((), (), s32[]{:S(2)}) async-start(), calls=%async_computation.11 | async-start | bytes 3981312 | tf_op jit(solution)/shard_map/all_gather | solution.py:85
  7.9 268.6 %all-gather.10.cloned.1.call-start = ((), (), s32[]{:S(2)}) async-start(), calls=%async_computation.5 | async-start | bytes 1769472 | tf_op jit(solution)/shard_map/all_gather | solution.py:94
  8.7 307.8 %reduce-scatter.6.cloned.1.call-start = ((), (), s32[]{:S(2)}) async-start(), calls=%async_computation.6 | async-start | bytes 245760 | tf_op jit(solution)/shard_map/reduce_scatter | solution.py:123
  13.5 269.7 %copy-start.3 = (bf16[1,1,154,384]{2,3,1,0:T(8,128)(2,1)}, bf16[1,1,154,384]{2,3,1,0:T(8,128)(2,1)S(1)}, u32[]{:S(2)}) copy-start(bf16[1,1,154,384]{2,3,1,0:T(8,128)(2,1)S(1)} %copy.106) | copy-start | bytes 354820
  29.6 246.9 %copy-start.34 = (pred[8,4]{1,0:T(8,128)(4,1)}, pred[8,4]{1,0:T(8,128)(4,1)S(1)}, u32[]{:S(2)}) copy-start(pred[8,4]{1,0:T(8,128)(4,1)S(1)} %fusion.204) | copy-start | bytes 100
  293.2 160.1 %reduce-scatter.8.cloned.1.call-start = ((), (), s32[]{:S(2)}) async-start(), calls=%async_computation.7 | async-start | bytes 245760 | tf_op jit(solution)/shard_map/reduce_scatter | solution.py:123
  317.3 3.9 collective-permute-start
  333.5 69.6 %copy-start.1 = (bf16[8,2,128,384]{3,2,1,0:T(8,128)(2,1)S(1)}, bf16[8,2,128,384]{3,2,1,0:T(8,128)(2,1)}, u32[]{:S(2)}) copy-start(bf16[8,2,128,384]{3,2,1,0:T(8,128)(2,1)} %all-gather.10.cloned.1.call-done) | copy-start | bytes 4718596
  333.5 69.6 %copy-start.35 = (pred[8,4]{1,0:T(8,128)(4,1)S(1)}, pred[8,4]{1,0:T(8,128)(4,1)}, u32[]{:S(2)}) copy-start(pred[8,4]{1,0:T(8,128)(4,1)} %copy-done.34) | copy-start | bytes 100
  333.6 69.6 %copy-start.39 = (pred[8,4]{1,0:T(8,128)(4,1)S(1)}, pred[8,4]{1,0:T(8,128)(4,1)}, u32[]{:S(2)}) copy-start(pred[8,4]{1,0:T(8,128)(4,1)} %fusion.205) | copy-start | bytes 100
  426.2 166.7 %reduce-scatter.10.cloned.1.call-start = ((), (), s32[]{:S(2)}) async-start(), calls=%async_computation.8 | async-start | bytes 245760 | tf_op jit(solution)/shard_map/reduce_scatter | solution.py:123
  454.7 5.3 collective-permute-start.1
  565.9 167.3 %reduce-scatter.12.cloned.1.call-start = ((), (), s32[]{:S(2)}) async-start(), calls=%async_computation.9 | async-start | bytes 245760 | tf_op jit(solution)/shard_map/reduce_scatter | solution.py:123
  594.4 5.1 collective-permute-start.2
  706.1 157.4 %reduce-scatter.14.cloned.1.call-start = ((), (), s32[]{:S(2)}) async-start(), calls=%async_computation.10 | async-start | bytes 245760 | tf_op jit(solution)/shard_map/reduce_scatter | solution.py:123
  734.6 4.9 collective-permute-start.3
  752.7 69.4 %copy-start.7 = (bf16[16,32,384]{2,1,0:T(8,128)(2,1)S(1)}, bf16[16,32,384]{2,1,0:T(8,128)(2,1)}, u32[]{:S(2)}) copy-start(bf16[16,32,384]{2,1,0:T(8,128)(2,1)} %copy-done.5) | copy-start | bytes 1179652
  752.7 69.4 %copy-start.9 = (bf16[16,32,384]{2,1,0:T(8,128)(2,1)S(1)}, bf16[16,32,384]{2,1,0:T(8,128)(2,1)}, u32[]{:S(2)}) copy-start(bf16[16,32,384]{2,1,0:T(8,128)(2,1)} %copy-done.8) | copy-start | bytes 1179652
  752.7 69.4 %copy-start.38 = (pred[8,4]{1,0:T(8,128)(4,1)S(1)}, pred[8,4]{1,0:T(8,128)(4,1)}, u32[]{:S(2)}) copy-start(pred[8,4]{1,0:T(8,128)(4,1)} %copy-done.34) | copy-start | bytes 100
  752.7 69.4 %copy-start.42 = (pred[8,4]{1,0:T(8,128)(4,1)S(1)}, pred[8,4]{1,0:T(8,128)(4,1)}, u32[]{:S(2)}) copy-start(pred[8,4]{1,0:T(8,128)(4,1)} %fusion.205) | copy-start | bytes 100
  752.7 69.4 %copy-start.46 = (pred[8,4]{1,0:T(8,128)(4,1)S(1)}, pred[8,4]{1,0:T(8,128)(4,1)}, u32[]{:S(2)}) copy-start(pred[8,4]{1,0:T(8,128)(4,1)} %fusion.206) | copy-start | bytes 100
  752.7 69.4 %copy-start.50 = (pred[8,4]{1,0:T(8,128)(4,1)S(1)}, pred[8,4]{1,0:T(8,128)(4,1)}, u32[]{:S(2)}) copy-start(pred[8,4]{1,0:T(8,128)(4,1)} %fusion.207) | copy-start | bytes 100
  865.3 3.2 collective-permute-start.4
  (48 other events, 1047.5 us)
Sparse Core Ops, SparseCore 0:
  11.2 162.6 all-gather.11
  177.1 99.3 all-gather.9
  293.3 23.0 reduce-scatter.5
  426.4 26.8 reduce-scatter.7
  566.0 26.8 reduce-scatter.9
  706.2 26.9 reduce-scatter.11
  836.6 26.8 reduce-scatter.13
where the time goes:
time: 894 us; the launch traced here: 891 us
  blocking collectives  390 us (44%)
  waiting for transfers between devices  305 us (34%)
  local copies, waits for them, and re-layouts  63.6 us (7%)
  matrix products  56.2 us (6%)
  other arithmetic  41.2 us (5%)
  between operations  26 us (3%)
    all_gather x5, blocking collectives, take_fresh(): arrived = lax.all_gather(new_kv_rows[None], 'seq', axis=0, tiled=True)  316 us
    all_gather x1, waiting for transfers between devices, body(): lax.all_gather(w_qkv[0], 'seq', axis=0, tiled=True)  144 us
    reduce_scatter x5, waiting for transfers between devices, body(): lax.psum_scatter(partial_value, 'tp', scatter_dimension=1, tiled=True)  121 us
    all_gather x5, blocking collectives, body(): full_rows = lax.all_gather(current, 'tp', axis=1, tiled=True)  60.4 us
    all_gather x1, waiting for transfers between devices, body(): lax.all_gather(stale_kv, 'seq', axis=0, tiled=True)  38.7 us
  transfers between devices with their start and end apart: 12, of which 8 were waited for; matrix products, arithmetic and copies ran while one was open for 4% of the time, Pallas kernels for 0%

commit v1 on v0

--- a/solution.py
+++ b/solution.py
@@ -5,6 +5,11 @@
 
 HEAD = 64
 MICRO = 4
+
+
+def exchange_gather(x, name, along):
+    sent = jnp.stack([x] * lax.axis_size(name))
+    return jnp.concatenate(lax.all_to_all(sent, name, 0, 0), axis=along)
 
 
 def from_behind(value, axis, steps):
@@ -51,7 +56,7 @@
 
 
 def take_fresh(new_kv_rows, column, is_valid, buffer, micro_ids):
-    arrived = lax.all_gather(new_kv_rows[None], "seq", axis=0, tiled=True)
+    arrived = exchange_gather(new_kv_rows[None], "seq", 0)
     hit_mask = (column[:, None] == micro_ids[None, :]) & is_valid
     return jnp.where(hit_mask[:, None, :, None, None], arrived[:, :, None], buffer)
 

time: 894 us -> 757 us (0.85)
  blocking collectives: 390 us -> 73.8 us
  waiting for transfers between devices: 305 us -> 403 us
  starting transfers between devices: 8.51 us -> 74 us
    all_gather x5 -> x0, blocking collectives: 316 us -> none  [take_fresh(): arrived = lax.all_gather(new_kv_rows[None], 'seq', axis=0, tiled=True)]
    all_to_all x0 -> x5, starting transfers between devices: none -> 65.7 us  [exchange_gather(): return jnp.concatenate(lax.all_to_all(sent, name, 0, 0), axis=along)]
    all_gather x1, waiting for transfers between devices: 38.7 us -> 96.5 us  [body(): lax.all_gather(stale_kv, 'seq', axis=0, tiled=True)]
    all_to_all x0 -> x5, waiting for transfers between devices: none -> 44.9 us  [exchange_gather(): return jnp.concatenate(lax.all_to_all(sent, name, 0, 0), axis=along)]
  transfers between devices with their start and end apart: 12 -> 17, of which waited for: 8 -> 12; matrix products, arithmetic and copies ran while one was open for 4% -> 6% of each run, Pallas kernels for 0% -> 0%
where the time goes in v1:
time: 757 us; the launch traced here: 753 us
  waiting for transfers between devices  403 us (53%)
  starting transfers between devices  74 us (10%)
  blocking collectives  73.8 us (10%)
  local copies, waits for them, and re-layouts  70 us (9%)
  matrix products  60.3 us (8%)
  other arithmetic  46.6 us (6%)
  between operations  25.7 us (3%)
    all_gather x1, waiting for transfers between devices, body(): lax.all_gather(w_qkv[0], 'seq', axis=0, tiled=True)  147 us
    reduce_scatter x5, waiting for transfers between devices, body(): lax.psum_scatter(partial_value, 'tp', scatter_dimension=1, tiled=True)  113 us
    all_gather x1, waiting for transfers between devices, body(): lax.all_gather(stale_kv, 'seq', axis=0, tiled=True)  96.5 us
    all_to_all x5, starting transfers between devices, exchange_gather(): return jnp.concatenate(lax.all_to_all(sent, name, 0, 0), axis=along)  65.7 us
    all_gather x5, blocking collectives, body(): full_rows = lax.all_gather(current, 'tp', axis=1, tiled=True)  60.4 us
    all_to_all x5, waiting for transfers between devices, exchange_gather(): return jnp.concatenate(lax.all_to_all(sent, name, 0, 0), axis=along)  44.9 us
    another operation x5, local copies, waits for them, and re-layouts, body(): all_keys = buffer[:, 0].reshape(-1, heads_here, HEAD)  17 us
    dot_general x5, matrix products, body(): jnp.dot(normed, projection, preferred_element_type=jnp.float32)  15.6 us
  transfers between devices with their start and end apart: 17, of which 12 were waited for; matrix products, arithmetic and copies ran while one was open for 6% of the time, Pallas kernels for 0%

profile of v1, /device:TPU:8, one launch (start us, length us, event | category | flops | bytes accessed | tf_op | source)
XLA Modules:
  0.0 753.4 jit_solution(7417442018095485374)
XLA Ops:
  13.2 12.3 %all-gather = bf16[1,32,1536]{2,1,0:T(8,128)(2,1)S(1)} all-gather(bf16[1,32,384]{2,1,0:T(8,128)(2,1)S(1)} %dynamic-slice_select_fusion), channel_id=2, replica_groups=mesh['req'=8,'section'=2,'seq'=8,'tp'=4] {'tp'}, dimensions={2}, use_global_device_ids=true | all-gather | bytes 122880 | tf_op jit(solution)/shard_map/all_gather | solution.py:114
  27.2 146.7 %all-gather.7.cloned.1.call-done = bf16[1,1536,3,384]{3,1,2,0:T(8,128)(2,1)} async-done(((bf16[1,192,3,384]{3,1,2,0:T(8,128)(2,1)}), bf16[1,1536,3,384]{3,1,2,0:T(8,128)(2,1)}) %all-gather.7.cloned.1.call-update) | async-done | bytes 3538960 | tf_op jit(solution)/shard_map/all_gather | solution.py:90
  173.9 6.1 copy.96
  183.9 5.1 all-to-all-start
  191.6 96.5 %all-gather.5.cloned.1.call-done = bf16[8,2,128,384]{3,2,1,0:T(8,128)(2,1)} async-done(((bf16[1,2,128,384]{3,2,1,0:T(8,128)(2,1)}), bf16[8,2,128,384]{3,2,1,0:T(8,128)(2,1)}) %all-gather.5.cloned.1.call-update) | async-done | bytes 1572880 | tf_op jit(solution)/shard_map/all_gather | solution.py:99
  306.7 19.2 %reduce-scatter.6.cloned.1.call-done = f32[32,384]{1,0:T(8,128)} async-done(((f32[32,1536]{1,0:T(8,128)}), f32[32,384]{1,0:T(8,128)}) %reduce-scatter.6.cloned.1.call-update) | async-done | bytes 49168 | tf_op jit(solution)/shard_map/reduce_scatter | solution.py:128
  330.8 12.0 %all_gather.27 = bf16[32,1536]{1,0:T(8,128)(2,1)S(1)} all-gather(bf16[32,384]{1,0:T(8,128)(2,1)S(1)} %bitcast_select_fusion), channel_id=1, replica_groups=mesh['req'=8,'section'=2,'seq'=8,'tp'=4] {'tp'}, dimensions={1}, use_global_device_ids=true | all-gather | bytes 122880 | tf_op jit(solution)/shard_map/all_gather | solution.py:114
  347.7 15.2 %all-to-all-start.1 = ((bf16[8,1,2,32,384]{4,3,2,1,0:T(8,128)(2,1)}), bf16[8,1,2,32,384]{4,3,2,1,0:T(8,128)(2,1)S(1)}, u32[]{:S(2)}, u32[]{:S(2)}) async-start(bf16[8,1,2,32,384]{4,3,2,1,0:T(8,128)(2,1)} %stack.67), calls=%async_computation.2 | async-start | bytes 786432 | tf_op jit(solution)/shard_map/all_to_all | solution.py:12
  368.1 11.8 %all-to-all-done.1 = bf16[8,1,2,32,384]{4,3,2,1,0:T(8,128)(2,1)S(1)} async-done(((bf16[8,1,2,32,384]{4,3,2,1,0:T(8,128)(2,1)}), bf16[8,1,2,32,384]{4,3,2,1,0:T(8,128)(2,1)S(1)}, u32[]{:S(2)}, u32[]{:S(2)}) %all-to-all-start.1) | async-done | bytes 393248 | tf_op jit(solution)/shard_map/all_to_all | solution.py:12
  391.0 3.7 reshape_squeeze.40
  401.1 24.0 %reduce-scatter.8.cloned.1.call-done = f32[32,384]{1,0:T(8,128)} async-done(((f32[32,1536]{1,0:T(8,128)}), f32[32,384]{1,0:T(8,128)}) %reduce-scatter.8.cloned.1.call-update) | async-done | bytes 49168 | tf_op jit(solution)/shard_map/reduce_scatter | solution.py:128
  432.1 12.0 %all_gather.28 = bf16[32,1536]{1,0:T(8,128)(2,1)S(1)} all-gather(bf16[32,384]{1,0:T(8,128)(2,1)S(1)} %bitcast_select_fusion.1), channel_id=1, replica_groups=mesh['req'=8,'section'=2,'seq'=8,'tp'=4] {'tp'}, dimensions={1}, use_global_device_ids=true | all-gather | bytes 122880 | tf_op jit(solution)/shard_map/all_gather | solution.py:114
  449.0 15.1 %all-to-all-start.2 = ((bf16[8,1,2,32,384]{4,3,2,1,0:T(8,128)(2,1)}), bf16[8,1,2,32,384]{4,3,2,1,0:T(8,128)(2,1)}, u32[]{:S(2)}, u32[]{:S(2)}) async-start(bf16[8,1,2,32,384]{4,3,2,1,0:T(8,128)(2,1)} %stack.71), calls=%async_computation.4 | async-start | bytes 786432 | tf_op jit(solution)/shard_map/all_to_all | solution.py:12
  469.3 11.9 %all-to-all-done.2 = bf16[8,1,2,32,384]{4,3,2,1,0:T(8,128)(2,1)} async-done(((bf16[8,1,2,32,384]{4,3,2,1,0:T(8,128)(2,1)}), bf16[8,1,2,32,384]{4,3,2,1,0:T(8,128)(2,1)}, u32[]{:S(2)}, u32[]{:S(2)}) %all-to-all-start.2) | async-done | bytes 393248 | tf_op jit(solution)/shard_map/all_to_all | solution.py:12
  503.3 24.1 %reduce-scatter.10.cloned.1.call-done = f32[32,384]{1,0:T(8,128)} async-done(((f32[32,1536]{1,0:T(8,128)}), f32[32,384]{1,0:T(8,128)}) %reduce-scatter.10.cloned.1.call-update) | async-done | bytes 49168 | tf_op jit(solution)/shard_map/reduce_scatter | solution.py:128
  534.7 12.2 %all_gather.29 = bf16[32,1536]{1,0:T(8,128)(2,1)S(1)} all-gather(bf16[32,384]{1,0:T(8,128)(2,1)S(1)} %bitcast_select_fusion.2), channel_id=1, replica_groups=mesh['req'=8,'section'=2,'seq'=8,'tp'=4] {'tp'}, dimensions={1}, use_global_device_ids=true | all-gather | bytes 122880 | tf_op jit(solution)/shard_map/all_gather | solution.py:114
  551.8 15.1 %all-to-all-start.3 = ((bf16[8,1,2,32,384]{4,3,2,1,0:T(8,128)(2,1)}), bf16[8,1,2,32,384]{4,3,2,1,0:T(8,128)(2,1)}, u32[]{:S(2)}, u32[]{:S(2)}) async-start(bf16[8,1,2,32,384]{4,3,2,1,0:T(8,128)(2,1)} %stack.75), calls=%async_computation.6 | async-start | bytes 786432 | tf_op jit(solution)/shard_map/all_to_all | solution.py:12
  572.0 11.6 %all-to-all-done.3 = bf16[8,1,2,32,384]{4,3,2,1,0:T(8,128)(2,1)} async-done(((bf16[8,1,2,32,384]{4,3,2,1,0:T(8,128)(2,1)}), bf16[8,1,2,32,384]{4,3,2,1,0:T(8,128)(2,1)}, u32[]{:S(2)}, u32[]{:S(2)}) %all-to-all-start.3) | async-done | bytes 393248 | tf_op jit(solution)/shard_map/all_to_all | solution.py:12
  606.3 24.1 %reduce-scatter.12.cloned.1.call-done = f32[32,384]{1,0:T(8,128)} async-done(((f32[32,1536]{1,0:T(8,128)}), f32[32,384]{1,0:T(8,128)}) %reduce-scatter.12.cloned.1.call-update) | async-done | bytes 49168 | tf_op jit(solution)/shard_map/reduce_scatter | solution.py:128
  637.7 12.0 %all_gather.30 = bf16[32,1536]{1,0:T(8,128)(2,1)S(1)} all-gather(bf16[32,384]{1,0:T(8,128)(2,1)S(1)} %bitcast_select_fusion.3), channel_id=1, replica_groups=mesh['req'=8,'section'=2,'seq'=8,'tp'=4] {'tp'}, dimensions={1}, use_global_device_ids=true | all-gather | bytes 122880 | tf_op jit(solution)/shard_map/all_gather | solution.py:114
  654.6 15.1 %all-to-all-start.4 = ((bf16[8,1,2,32,384]{4,3,2,1,0:T(8,128)(2,1)}), bf16[8,1,2,32,384]{4,3,2,1,0:T(8,128)(2,1)}, u32[]{:S(2)}, u32[]{:S(2)}) async-start(bf16[8,1,2,32,384]{4,3,2,1,0:T(8,128)(2,1)} %stack.79), calls=%async_computation.8 | async-start | bytes 786432 | tf_op jit(solution)/shard_map/all_to_all | solution.py:12
  676.6 9.6 %all-to-all-done.4 = bf16[8,1,2,32,384]{4,3,2,1,0:T(8,128)(2,1)} async-done(((bf16[8,1,2,32,384]{4,3,2,1,0:T(8,128)(2,1)}), bf16[8,1,2,32,384]{4,3,2,1,0:T(8,128)(2,1)}, u32[]{:S(2)}, u32[]{:S(2)}) %all-to-all-start.4) | async-done | bytes 393248 | tf_op jit(solution)/shard_map/all_to_all | solution.py:12
  704.1 21.9 %reduce-scatter.14.cloned.1.call-done = f32[32,384]{1,0:T(8,128)} async-done(((f32[32,1536]{1,0:T(8,128)}), f32[32,384]{1,0:T(8,128)}) %reduce-scatter.14.cloned.1.call-update) | async-done | bytes 49168 | tf_op jit(solution)/shard_map/reduce_scatter | solution.py:128
  731.8 13.3 %all_gather.31 = bf16[128,1536]{1,0:T(8,128)(2,1)S(1)} all-gather(bf16[128,384]{1,0:T(8,128)(2,1)S(1)} %bitcast.236), channel_id=1, replica_groups=mesh['req'=8,'section'=2,'seq'=8,'tp'=4] {'tp'}, dimensions={1}, use_global_device_ids=true | all-gather | bytes 491520 | tf_op jit(solution)/shard_map/all_gather | solution.py:134
  (286 shorter events, 177.1 us)
Async XLA Ops:
  7.2 297.8 %copy-start = (bf16[1,384,1536]{2,1,0:T(8,128)(2,1)S(1)}, bf16[1,384,1536]{2,1,0:T(8,128)(2,1)}, u32[]{:S(2)}) copy-start(bf16[1,384,1536]{2,1,0:T(8,128)(2,1)} %param.15) | copy-start | bytes 3538948
  7.2 166.7 %all-gather.7.cloned.1.call-start = ((), (), s32[]{:S(2)}) async-start(), calls=%async_computation.16 | async-start | bytes 3981312 | tf_op jit(solution)/shard_map/all_gather | solution.py:90
  7.9 280.1 %all-gather.5.cloned.1.call-start = ((), (), s32[]{:S(2)}) async-start(), calls=%async_computation.10 | async-start | bytes 1769472 | tf_op jit(solution)/shard_map/all_gather | solution.py:99
  183.9 104.1 %all-to-all-start = ((bf16[8,1,2,32,384]{4,3,2,1,0:T(8,128)(2,1)}), bf16[8,1,2,32,384]{4,3,2,1,0:T(8,128)(2,1)S(1)}, u32[]{:S(2)}, u32[]{:S(2)}) async-start(bf16[8,1,2,32,384]{4,3,2,1,0:T(8,128)(2,1)} %stack.63), calls=%async_computation | async-start | bytes 786432 | tf_op jit(solution)/shard_map/all_to_all | solution.py:12
  189.0 136.8 %reduce-scatter.6.cloned.1.call-start = ((), (), s32[]{:S(2)}) async-start(), calls=%async_computation.11 | async-start | bytes 245760 | tf_op jit(solution)/shard_map/reduce_scatter | solution.py:128
  189.6 100.4 %copy-start.3 = (bf16[1,1,154,384]{2,3,1,0:T(8,128)(2,1)}, bf16[1,1,154,384]{2,3,1,0:T(8,128)(2,1)S(1)}, u32[]{:S(2)}) copy-start(bf16[1,1,154,384]{2,3,1,0:T(8,128)(2,1)S(1)} %copy.101) | copy-start | bytes 354820
  191.1 98.8 %copy-start.39 = (pred[154]{0:T(512)(128)(4,1)}, pred[154]{0:T(512)(128)(4,1)S(1)}, u32[]{:S(2)}) copy-start(pred[154]{0:T(512)(128)(4,1)S(1)} %iota_compare_fusion.5) | copy-start | bytes 466
  191.2 98.7 %copy-start.32 = (pred[8,4]{1,0:T(8,128)(4,1)}, pred[8,4]{1,0:T(8,128)(4,1)S(1)}, u32[]{:S(2)}) copy-start(pred[8,4]{1,0:T(8,128)(4,1)S(1)} %fusion.204) | copy-start | bytes 100
  326.7 4.1 collective-permute-start
  346.3 33.6 %copy-start.1 = (bf16[8,2,128,384]{3,2,1,0:T(8,128)(2,1)S(1)}, bf16[8,2,128,384]{3,2,1,0:T(8,128)(2,1)}, u32[]{:S(2)}) copy-start(bf16[8,2,128,384]{3,2,1,0:T(8,128)(2,1)} %all-gather.5.cloned.1.call-done) | copy-start | bytes 4718596
  347.7 32.2 %all-to-all-start.1 = ((bf16[8,1,2,32,384]{4,3,2,1,0:T(8,128)(2,1)}), bf16[8,1,2,32,384]{4,3,2,1,0:T(8,128)(2,1)S(1)}, u32[]{:S(2)}, u32[]{:S(2)}) async-start(bf16[8,1,2,32,384]{4,3,2,1,0:T(8,128)(2,1)} %stack.67), calls=%async_computation.2 | async-start | bytes 786432 | tf_op jit(solution)/shard_map/all_to_all | solution.py:12
  362.9 62.2 %reduce-scatter.8.cloned.1.call-start = ((), (), s32[]{:S(2)}) async-start(), calls=%async_computation.12 | async-start | bytes 245760 | tf_op jit(solution)/shard_map/reduce_scatter | solution.py:128
  426.5 4.9 collective-permute-start.1
  449.0 32.1 %all-to-all-start.2 = ((bf16[8,1,2,32,384]{4,3,2,1,0:T(8,128)(2,1)}), bf16[8,1,2,32,384]{4,3,2,1,0:T(8,128)(2,1)}, u32[]{:S(2)}, u32[]{:S(2)}) async-start(bf16[8,1,2,32,384]{4,3,2,1,0:T(8,128)(2,1)} %stack.71), calls=%async_computation.4 | async-start | bytes 786432 | tf_op jit(solution)/shard_map/all_to_all | solution.py:12
  464.2 63.2 %reduce-scatter.10.cloned.1.call-start = ((), (), s32[]{:S(2)}) async-start(), calls=%async_computation.13 | async-start | bytes 245760 | tf_op jit(solution)/shard_map/reduce_scatter | solution.py:128
  528.8 5.1 collective-permute-start.2
  551.8 31.8 %all-to-all-start.3 = ((bf16[8,1,2,32,384]{4,3,2,1,0:T(8,128)(2,1)}), bf16[8,1,2,32,384]{4,3,2,1,0:T(8,128)(2,1)}, u32[]{:S(2)}, u32[]{:S(2)}) async-start(bf16[8,1,2,32,384]{4,3,2,1,0:T(8,128)(2,1)} %stack.75), calls=%async_computation.6 | async-start | bytes 786432 | tf_op jit(solution)/shard_map/all_to_all | solution.py:12
  566.9 63.5 %reduce-scatter.12.cloned.1.call-start = ((), (), s32[]{:S(2)}) async-start(), calls=%async_computation.14 | async-start | bytes 245760 | tf_op jit(solution)/shard_map/reduce_scatter | solution.py:128
  631.8 5.1 collective-permute-start.3
  654.6 31.6 %all-to-all-start.4 = ((bf16[8,1,2,32,384]{4,3,2,1,0:T(8,128)(2,1)}), bf16[8,1,2,32,384]{4,3,2,1,0:T(8,128)(2,1)}, u32[]{:S(2)}, u32[]{:S(2)}) async-start(bf16[8,1,2,32,384]{4,3,2,1,0:T(8,128)(2,1)} %stack.79), calls=%async_computation.8 | async-start | bytes 786432 | tf_op jit(solution)/shard_map/all_to_all | solution.py:12
  669.7 56.3 %reduce-scatter.14.cloned.1.call-start = ((), (), s32[]{:S(2)}) async-start(), calls=%async_computation.15 | async-start | bytes 245760 | tf_op jit(solution)/shard_map/reduce_scatter | solution.py:128
  701.6 44.0 %copy-start.47 = (bf16[1536,8]{0,1:T(8,128)(2,1)S(1)}, bf16[1536,8]{0,1:T(8,128)(2,1)}, u32[]{:S(2)}) copy-start(bf16[1536,8]{0,1:T(8,128)(2,1)} %param.18) | copy-start | bytes 73732
  701.6 44.0 %copy-start.48 = (f32[128,8]{0,1:T(8,128)S(1)}, f32[128,8]{0,1:T(8,128)}, u32[]{:S(2)}) copy-start(f32[128,8]{0,1:T(8,128)} %param.13) | copy-start | bytes 12292
  727.7 3.2 collective-permute-start.4
  (42 other events, 422.8 us)
Sparse Core Ops, SparseCore 0:
  11.1 162.7 all-gather.6
  177.1 110.9 all-gather.4
  306.1 19.7 reduce-scatter.5
  401.2 23.8 reduce-scatter.7
  503.4 23.9 reduce-scatter.9
  606.4 23.9 reduce-scatter.11
  701.7 24.2 reduce-scatter.13
